TPU v7x, 512 devices: a whole 4x4x16 slice. The times are simulated.
512 devices in a mesh: tm: 128 (over x_lo, z, y), feat: 4 (over x_hi, core).
Axes of the slice: x: 4 (x_hi: 2, x_lo: 2; x = x_hi * 2 + x_lo), y: 4, z: 16, core: 2. Of those that a mesh axis runs over, the one named last changes fastest.
Arguments:
- frames: bfloat16 [4096, 2048], P('tm'), may hold values from -6 to 6
- frequency: bfloat16 [2048, 4096], P(None, 'feat'), may hold values from -0.125 to 0.125
- phases: float32 [4096], P('feat'), may hold values from -3.140625 to 3.140625
Outputs:
- instant_tiles: float32 [128, 4, 128, 256], P('tm', 'feat')
- lagged_tiles: float32 [128, 4, 128, 256], P('tm', 'feat')
All inputs are finite; a program needn't handle non-finite values.
Results may differ from a plain program's by a relative error of at most 0.0003.
Values may be sent and summed in bfloat16 or wider, within the bound.
A program may use at most 64 MiB of HBM per device.

v0:
```python
import math
import jax
import jax.numpy as jnp
from jax import lax
from jax.sharding import PartitionSpec as P

LAG = 512
ROW_SPLIT = 8
SCALE = math.sqrt(2.0)


def shards(frames, frequency, phases):
    tm_count = lax.axis_size("tm")
    feat_count = lax.axis_size("feat")
    projected = jnp.dot(frames, frequency, preferred_element_type=jnp.float32) + phases[None, :]
    local_feats = (SCALE * jnp.cos(projected)).astype(jnp.bfloat16)
    frame_count, local_width = local_feats.shape
    feat_width = local_width * feat_count
    tile_rows = feat_width // (feat_count * ROW_SPLIT)
    tile_cols = feat_width * ROW_SPLIT // tm_count
    col_groups = tm_count // ROW_SPLIT
    frame_total = frame_count * tm_count
    all_feats = lax.all_gather(local_feats, "feat", axis=1, tiled=True)
    row_parts = local_feats.reshape(frame_count, ROW_SPLIT, tile_rows).transpose(1, 0, 2)
    row_send = jnp.broadcast_to(row_parts[None], (col_groups, ROW_SPLIT, frame_count, tile_rows))
    row_send = row_send.reshape(tm_count, frame_count, tile_rows)
    row_recv = lax.all_to_all(row_send, "tm", split_axis=0, concat_axis=0, tiled=True).reshape(
        frame_total, tile_rows
    )
    head_rows = row_recv[: frame_total - LAG]
    row_total = all_feats.shape[0]
    col_parts = all_feats.reshape(row_total, col_groups, tile_cols).transpose(1, 0, 2)
    spread_out = jnp.broadcast_to(col_parts[:, None], (col_groups, ROW_SPLIT, row_total, tile_cols))
    received = lax.all_to_all(
        spread_out.reshape(tm_count, row_total, tile_cols),
        "tm",
        split_axis=0,
        concat_axis=0,
        tiled=True,
    )
    col_data = received.reshape(frame_total, received.shape[2])
    instant = (
        jnp.einsum("sr,sc->rc", row_recv, col_data, preferred_element_type=jnp.float32)
        / frame_total
    )
    lagged = jnp.einsum(
        "sr,sc->rc", head_rows, col_data[LAG:], preferred_element_type=jnp.float32
    ) / (frame_total - LAG)
    instant, lagged = (instant, lagged)
    return (instant.reshape(1, 1, tile_rows, tile_cols), lagged.reshape(1, 1, tile_rows, tile_cols))


def solution(mesh):
    placed = (P("tm", None), P(None, "feat"), P("feat"))
    return jax.shard_map(
        shards,
        mesh=mesh,
        in_specs=placed,
        out_specs=(P("tm", "feat", None, None), P("tm", "feat", None, None)),
        check_vma=False,
    )
```

profile of v0, /device:TPU:4, one launch (start us, length us, event | category | flops | bytes accessed | tf_op | source)
XLA Modules:
  0.0 197.1 jit_solution(6521872163242553725)
XLA Ops:
  0.6 0.0 copy-start
  0.6 0.9 copy-done
  1.5 3.4 %fusion.15 = bf16[32,1024]{1,0:T(8,128)(2,1)S(1)} fusion(bf16[32,2048]{1,0:T(8,128)(2,1)S(1)} %copy-done, bf16[2048,1024]{1,0:T(8,128)(2,1)} %param.4, f32[1024]{0:T(1024)} %param.5), kind=kOutput, calls=%fused_computation.11 | convolution fusion | flops 134316032 | bytes 4395008 | tf_op jit(solution)/shard_map/dot_general | solution.py:15
  5.0 1.2 broadcast_in_dim.4
  6.2 20.6 %all-to-all-start = ((bf16[128,32,128]{2,1,0:T(8,128)(2,1)}), bf16[128,32,128]{2,1,0:T(8,128)(2,1)S(1)}, u32[]{:S(2)}, u32[]{:S(2)}) async-start(bf16[128,32,128]{2,1,0:T(8,128)(2,1)} %bitcast.1), calls=%async_computation | async-start | bytes 2097152 | tf_op jit(solution)/shard_map/all_to_all | solution.py:27
  26.8 7.5 %all_gather.3 = bf16[32,4096]{1,0:T(8,128)(2,1)S(1)} all-gather(bf16[32,1024]{1,0:T(8,128)(2,1)S(1)} %fusion.15), channel_id=1, replica_groups=mesh['tm'=128,'feat'=4] {'feat'}, dimensions={1}, use_global_device_ids=true | all-gather | bytes 327680 | tf_op jit(solution)/shard_map/all_gather | solution.py:23
  34.3 0.1 copy.11
  34.4 49.9 %all-to-all-done = bf16[128,32,128]{2,1,0:T(8,128)(2,1)S(1)} async-done(((bf16[128,32,128]{2,1,0:T(8,128)(2,1)}), bf16[128,32,128]{2,1,0:T(8,128)(2,1)S(1)}, u32[]{:S(2)}, u32[]{:S(2)}) %all-to-all-start) | async-done | bytes 1048608 | tf_op jit(solution)/shard_map/all_to_all | solution.py:27
  84.3 0.0 copy-start.1
  84.3 1.7 broadcast_in_dim.5
  86.0 6.2 %all-to-all-start.1 = ((bf16[128,32,256]{2,1,0:T(8,128)(2,1)}), bf16[128,32,256]{2,1,0:T(8,128)(2,1)S(1)}, u32[]{:S(2)}, u32[]{:S(2)}) async-start(bf16[128,32,256]{2,1,0:T(8,128)(2,1)} %bitcast.30), calls=%async_computation.1 | async-start | bytes 4194304 | tf_op jit(solution)/shard_map/all_to_all | solution.py:34
  92.2 0.0 copy-done.1
  92.2 0.0 slice-start
  92.2 100.4 %all-to-all-done.1 = bf16[128,32,256]{2,1,0:T(8,128)(2,1)S(1)} async-done(((bf16[128,32,256]{2,1,0:T(8,128)(2,1)}), bf16[128,32,256]{2,1,0:T(8,128)(2,1)S(1)}, u32[]{:S(2)}, u32[]{:S(2)}) %all-to-all-start.1) | async-done | bytes 2097184 | tf_op jit(solution)/shard_map/all_to_all | solution.py:34
  192.6 0.1 slice.11
  192.8 0.0 slice-done
  192.8 0.0 copy-start.2
  192.8 3.1 %fusion.12 = f32[1,1,128,256]{3,2,1,0:T(8,128)} fusion(bf16[112,32,256]{2,1,0:T(8,128)(2,1)S(1)} %slice.11, bf16[112,32,128]{2,1,0:T(8,128)(2,1)S(1)} %slice-done), kind=kOutput, calls=%fused_computation.10 | convolution fusion | flops 234913792 | bytes 2883584 | tf_op jit(solution)/shard_map/sr,sc->rc/dot_general | solution.py:46
  195.9 0.0 copy-done.2
  195.9 1.2 fusion.8
  (3 shorter events, 0.1 us)
Async XLA Ops:
  0.6 0.9 copy-start
  6.2 78.2 %all-to-all-start = ((bf16[128,32,128]{2,1,0:T(8,128)(2,1)}), bf16[128,32,128]{2,1,0:T(8,128)(2,1)S(1)}, u32[]{:S(2)}, u32[]{:S(2)}) async-start(bf16[128,32,128]{2,1,0:T(8,128)(2,1)} %bitcast.1), calls=%async_computation | async-start | bytes 2097152 | tf_op jit(solution)/shard_map/all_to_all | solution.py:27
  84.3 7.9 %copy-start.1 = (bf16[128,32,128]{2,1,0:T(8,128)(2,1)}, bf16[128,32,128]{2,1,0:T(8,128)(2,1)S(1)}, u32[]{:S(2)}) copy-start(bf16[128,32,128]{2,1,0:T(8,128)(2,1)S(1)} %all-to-all-done) | copy-start | bytes 3145732
  86.0 106.6 %all-to-all-start.1 = ((bf16[128,32,256]{2,1,0:T(8,128)(2,1)}), bf16[128,32,256]{2,1,0:T(8,128)(2,1)S(1)}, u32[]{:S(2)}, u32[]{:S(2)}) async-start(bf16[128,32,256]{2,1,0:T(8,128)(2,1)} %bitcast.30), calls=%async_computation.1 | async-start | bytes 4194304 | tf_op jit(solution)/shard_map/all_to_all | solution.py:34
  92.2 100.6 %slice-start = ((bf16[128,32,128]{2,1,0:T(8,128)(2,1)}), bf16[112,32,128]{2,1,0:T(8,128)(2,1)S(1)}, s32[]{:S(2)}) async-start(bf16[128,32,128]{2,1,0:T(8,128)(2,1)} %copy-done.1), calls=%async_computation.2 | async-start | bytes 1835008 | tf_op jit(solution)/shard_map/slice | solution.py:30
  192.8 3.1 %copy-start.2 = (bf16[128,32,128]{2,1,0:T(8,128)(2,1)S(1)}, bf16[128,32,128]{2,1,0:T(8,128)(2,1)}, u32[]{:S(2)}) copy-start(bf16[128,32,128]{2,1,0:T(8,128)(2,1)} %copy-done.1) | copy-start | bytes 3145732
where the time goes:
time: 197 us
  waiting for transfers between devices  150 us (76%)
  starting transfers between devices  26.8 us (14%)
  matrix products  7.72 us (4%)
  blocking collectives  7.49 us (4%)
  local copies, waits for them, and re-layouts  4.04 us (2%)
    all_to_all x1, waiting for transfers between devices, shards(): lax.all_to_all(spread_out.reshape(tm_count, row_total, tile_cols), 'tm',...  100 us
    all_to_all x1, waiting for transfers between devices, shards(): lax.all_to_all(row_send, 'tm', split_axis=0, concat_axis=0, tiled=True)  49.9 us
    all_to_all x1, starting transfers between devices, shards(): lax.all_to_all(row_send, 'tm', split_axis=0, concat_axis=0, tiled=True)  20.6 us
    all_gather x1, blocking collectives, shards(): all_feats = lax.all_gather(local_feats, 'feat', axis=1, tiled=True)  7.49 us
    all_to_all x1, starting transfers between devices, shards(): lax.all_to_all(spread_out.reshape(tm_count, row_total, tile_cols), 'tm',...  6.21 us
  transfers between devices with their start and end apart: 2, of which 2 were waited for; matrix products, arithmetic and copies ran while one was open for 0% of the time, Pallas kernels for 0%

commit v1 on v0

--- a/solution.py
+++ b/solution.py
@@ -20,7 +20,16 @@
     tile_cols = feat_width * ROW_SPLIT // tm_count
     col_groups = tm_count // ROW_SPLIT
     frame_total = frame_count * tm_count
-    all_feats = lax.all_gather(local_feats, "feat", axis=1, tiled=True)
+    pair_edge = lambda target, link_axis, where_dim: jnp.concatenate(
+        lax.all_to_all(
+            jnp.stack(lax.psum(1, axis_name=link_axis) * [target]),
+            axis_name=link_axis,
+            split_axis=0,
+            concat_axis=0,
+        ),
+        where_dim,
+    )
+    all_feats = pair_edge(local_feats, "feat", 1)
     row_parts = local_feats.reshape(frame_count, ROW_SPLIT, tile_rows).transpose(1, 0, 2)
     row_send = jnp.broadcast_to(row_parts[None], (col_groups, ROW_SPLIT, frame_count, tile_rows))
     row_send = row_send.reshape(tm_count, frame_count, tile_rows)

time: 197 us -> 208 us (1.056)
  the two profiles are of different devices: /device:TPU:4 before, /device:TPU:2 now
where the time goes in v1:
time: 208 us; the launch traced here: 207 us
  waiting for transfers between devices  162 us (78%)
  starting transfers between devices  31.8 us (15%)
  matrix products  7.72 us (4%)
  local copies, waits for them, and re-layouts  5.11 us (2%)
    all_to_all x1, waiting for transfers between devices, shards(): lax.all_to_all(spread_out.reshape(tm_count, row_total, tile_cols), 'tm',...  98.8 us
    all_to_all x1, waiting for transfers between devices, shards(): lax.all_to_all(row_send, 'tm', split_axis=0, concat_axis=0, tiled=True)  55.6 us
    all_to_all x1, starting transfers between devices, shards(): lax.all_to_all(row_send, 'tm', split_axis=0, concat_axis=0, tiled=True)  20.8 us
    all_to_all x1, starting transfers between devices, shards(): lax.all_to_all(spread_out.reshape(tm_count, row_total, tile_cols), 'tm',...  7.53 us
    all_to_all x1, waiting for transfers between devices, shards(): lax.all_to_all(jnp.stack(lax.psum(1, axis_name=link_axis) * [target]), ax...  7.48 us
  transfers between devices with their start and end apart: 3, of which 3 were waited for; matrix products, arithmetic and copies ran while one was open for 0% of the time, Pallas kernels for 0%

profile of v1, /device:TPU:2, one launch (start us, length us, event | category | flops | bytes accessed | tf_op | source)
XLA Modules:
  0.0 207.2 jit_solution(9749326742258321993)
XLA Ops:
  0.6 0.0 copy-start
  0.6 0.9 copy-done
  1.5 3.4 %fusion.15 = bf16[32,1024]{1,0:T(8,128)(2,1)S(1)} fusion(bf16[32,2048]{1,0:T(8,128)(2,1)S(1)} %copy-done, bf16[2048,1024]{1,0:T(8,128)(2,1)} %param.4, f32[1024]{0:T(1024)} %param.5), kind=kOutput, calls=%fused_computation.11 | convolution fusion | flops 134316032 | bytes 4395008 | tf_op jit(solution)/shard_map/dot_general | solution.py:15
  5.0 0.7 stack.2
  5.7 3.4 %all-to-all-start.1 = ((bf16[4,32,1024]{2,1,0:T(8,128)(2,1)}), bf16[4,32,1024]{2,1,0:T(8,128)(2,1)S(1)}, u32[]{:S(2)}, u32[]{:S(2)}) async-start(bf16[4,32,1024]{2,1,0:T(8,128)(2,1)} %stack.2), calls=%async_computation.1 | async-start | bytes 524288 | tf_op jit(solution)/shard_map/all_to_all | solution.py:24
  9.2 7.5 %all-to-all-done.1 = bf16[4,32,1024]{2,1,0:T(8,128)(2,1)S(1)} async-done(((bf16[4,32,1024]{2,1,0:T(8,128)(2,1)}), bf16[4,32,1024]{2,1,0:T(8,128)(2,1)S(1)}, u32[]{:S(2)}, u32[]{:S(2)}) %all-to-all-start.1) | async-done | bytes 262176 | tf_op jit(solution)/shard_map/all_to_all | solution.py:24
  16.6 1.2 broadcast_in_dim.4
  17.8 20.8 %all-to-all-start = ((bf16[128,32,128]{2,1,0:T(8,128)(2,1)}), bf16[128,32,128]{2,1,0:T(8,128)(2,1)S(1)}, u32[]{:S(2)}, u32[]{:S(2)}) async-start(bf16[128,32,128]{2,1,0:T(8,128)(2,1)} %bitcast.1), calls=%async_computation | async-start | bytes 2097152 | tf_op jit(solution)/shard_map/all_to_all | solution.py:36
  38.7 0.2 copy.16
  38.9 0.2 reshape_reshape.3
  39.1 0.1 copy.17
  39.2 55.6 %all-to-all-done = bf16[128,32,128]{2,1,0:T(8,128)(2,1)S(1)} async-done(((bf16[128,32,128]{2,1,0:T(8,128)(2,1)}), bf16[128,32,128]{2,1,0:T(8,128)(2,1)S(1)}, u32[]{:S(2)}, u32[]{:S(2)}) %all-to-all-start) | async-done | bytes 1048608 | tf_op jit(solution)/shard_map/all_to_all | solution.py:36
  94.7 0.0 copy-start.1
  94.7 1.6 broadcast_in_dim.5
  96.4 7.5 %all-to-all-start.2 = ((bf16[128,32,256]{2,1,0:T(8,128)(2,1)}), bf16[128,32,256]{2,1,0:T(8,128)(2,1)S(1)}, u32[]{:S(2)}, u32[]{:S(2)}) async-start(bf16[128,32,256]{2,1,0:T(8,128)(2,1)} %bitcast.28), calls=%async_computation.2 | async-start | bytes 4194304 | tf_op jit(solution)/shard_map/all_to_all | solution.py:43
  103.9 0.0 copy-done.1
  103.9 0.0 slice-start
  103.9 98.8 %all-to-all-done.2 = bf16[128,32,256]{2,1,0:T(8,128)(2,1)S(1)} async-done(((bf16[128,32,256]{2,1,0:T(8,128)(2,1)}), bf16[128,32,256]{2,1,0:T(8,128)(2,1)S(1)}, u32[]{:S(2)}, u32[]{:S(2)}) %all-to-all-start.2) | async-done | bytes 2097184 | tf_op jit(solution)/shard_map/all_to_all | solution.py:43
  202.7 0.1 slice.11
  202.9 0.0 slice-done
  202.9 0.0 copy-start.2
  202.9 3.1 %fusion.12 = f32[1,1,128,256]{3,2,1,0:T(8,128)} fusion(bf16[112,32,256]{2,1,0:T(8,128)(2,1)S(1)} %slice.11, bf16[112,32,128]{2,1,0:T(8,128)(2,1)S(1)} %slice-done), kind=kOutput, calls=%fused_computation.10 | convolution fusion | flops 234913792 | bytes 2883584 | tf_op jit(solution)/shard_map/sr,sc->rc/dot_general | solution.py:55
  206.0 0.0 copy-done.2
  206.0 1.2 fusion.8
  (2 shorter events, 0.0 us)
Async XLA Ops:
  0.6 0.9 copy-start
  5.7 10.9 %all-to-all-start.1 = ((bf16[4,32,1024]{2,1,0:T(8,128)(2,1)}), bf16[4,32,1024]{2,1,0:T(8,128)(2,1)S(1)}, u32[]{:S(2)}, u32[]{:S(2)}) async-start(bf16[4,32,1024]{2,1,0:T(8,128)(2,1)} %stack.2), calls=%async_computation.1 | async-start | bytes 524288 | tf_op jit(solution)/shard_map/all_to_all | solution.py:24
  17.8 76.9 %all-to-all-start = ((bf16[128,32,128]{2,1,0:T(8,128)(2,1)}), bf16[128,32,128]{2,1,0:T(8,128)(2,1)S(1)}, u32[]{:S(2)}, u32[]{:S(2)}) async-start(bf16[128,32,128]{2,1,0:T(8,128)(2,1)} %bitcast.1), calls=%async_computation | async-start | bytes 2097152 | tf_op jit(solution)/shard_map/all_to_all | solution.py:36
  94.7 9.2 %copy-start.1 = (bf16[128,32,128]{2,1,0:T(8,128)(2,1)}, bf16[128,32,128]{2,1,0:T(8,128)(2,1)S(1)}, u32[]{:S(2)}) copy-start(bf16[128,32,128]{2,1,0:T(8,128)(2,1)S(1)} %all-to-all-done) | copy-start | bytes 3145732
  96.4 106.3 %all-to-all-start.2 = ((bf16[128,32,256]{2,1,0:T(8,128)(2,1)}), bf16[128,32,256]{2,1,0:T(8,128)(2,1)S(1)}, u32[]{:S(2)}, u32[]{:S(2)}) async-start(bf16[128,32,256]{2,1,0:T(8,128)(2,1)} %bitcast.28), calls=%async_computation.2 | async-start | bytes 4194304 | tf_op jit(solution)/shard_map/all_to_all | solution.py:43
  103.9 98.9 %slice-start = ((bf16[128,32,128]{2,1,0:T(8,128)(2,1)}), bf16[112,32,128]{2,1,0:T(8,128)(2,1)S(1)}, s32[]{:S(2)}) async-start(bf16[128,32,128]{2,1,0:T(8,128)(2,1)} %copy-done.1), calls=%async_computation.3 | async-start | bytes 1835008 | tf_op jit(solution)/shard_map/slice | solution.py:39
  202.9 3.1 %copy-start.2 = (bf16[128,32,128]{2,1,0:T(8,128)(2,1)S(1)}, bf16[128,32,128]{2,1,0:T(8,128)(2,1)}, u32[]{:S(2)}) copy-start(bf16[128,32,128]{2,1,0:T(8,128)(2,1)} %copy-done.1) | copy-start | bytes 3145732
